TPU v7x, 1024 devices: a whole 4x4x32 slice. The times are simulated.
1024 devices in a mesh: fsdp: 16 (over y, z_hi), sample: 8 (over x, core), tp: 8 (over z_lo).
Axes of the slice: x: 4, y: 4, z: 32 (z_hi: 4, z_lo: 8; z = z_hi * 8 + z_lo), core: 2. Of those that a mesh axis runs over, the one named last changes fastest.
Arguments:
- hidden: bfloat16 [32, 128, 4, 4096], P('fsdp', 'sample'), may hold values from -6 to 6
- qkv_weight: bfloat16 [4096, 8, 768], P('fsdp', 'tp'), may hold values from -0.09375 to 0.09375
- qkv_bias: float32 [8, 768], P('tp'), may hold values from -6 to 6
- prompt_pool: bfloat16 [32, 48, 16, 8, 256], P('fsdp', 'sample', None, 'tp'), as said below
- block_table: int32 [32, 32], P('fsdp', 'sample'), may hold values from 0 to 5, as said below
- group_prompts: int32 [32], P('fsdp'), may hold values from 0 to 31, each once
- decode_len: int32 [32, 128], P('fsdp', 'sample'), may hold values from 1 to 4
Outputs:
- attn_out: bfloat16 [32, 128, 4, 8, 512], P('fsdp', 'sample', None, 'tp')
Inputs may be any that keep to these rules, and one draw needn't show every extreme that they name: `block_table`: for each prompt and each sample index s, the 4 entries in columns s * 4 to (s + 1) * 4 - 1 are distinct. `group_prompts`: each prompt is named by exactly one slot. `prompt_pool`: keys already carry their positions' rotation.
All inputs are finite; a program needn't handle non-finite values.
Results may differ from a plain program's by a relative error of at most 0.012.
Values may be sent and summed in bfloat16 or wider, within the bound.
No kernel may reach another device: no remote copies, remote signals or barrier semaphores. Data moves between devices by JAX's collectives and lax.ppermute only.
A program may use at most 32 MiB of HBM per device.

v0:
```python
import jax
import jax.numpy as jnp
import numpy as np
from jax import lax
from jax.experimental import pallas as pl
from jax.experimental.pallas import tpu as pltpu
from jax.sharding import Mesh, PartitionSpec as P


HD = 128
HEADS = 6
GROUP = 4
NY, NZ, NX, NC = 4, 4, 4, 2
SLOTS = 2
SAMPLES_DEV = 16
STEPS = 4
ROWS = SLOTS * SAMPLES_DEV * STEPS
WIDTH = 4096
K_SHARD = 256
W_ROWS = HEADS * HD // (NX * NC)
TOK = 64
C_ROWS = 2 * TOK
Z_ROWS = 2 * W_ROWS + SLOTS * C_ROWS
Y_ROWS = NZ * 2 * W_ROWS + SLOTS * C_ROWS
X_ROWS = W_ROWS + SLOTS * C_ROWS
PLEN = 512
INTERPRET = False


def vmem():
    return pl.BlockSpec(memory_space=pltpu.VMEM)


def smem():
    return pl.BlockSpec(memory_space=pltpu.SMEM)


def prep_kernel(place, table, w_ref, pool_ref, out_ref):
    wt = w_ref[...].T
    for k in range(NX * NC):

        @pl.when(place[0] * NC + place[1] == k)
        def _(k=k):
            for g in range(HEADS * 2):
                lo = g * 64 + k * 8
                for half in range(2):
                    out_ref[half * W_ROWS + g * 8 : half * W_ROWS + (g + 1) * 8, :] = wt[
                        lo : lo + 8, half * 128 : (half + 1) * 128
                    ]

    for i in range(SLOTS):
        for b in range(4):
            block = pool_ref[i, table[i, b]]
            base = 2 * W_ROWS + i * C_ROWS + b * 16
            out_ref[base : base + 16, :] = block[:, :HD]
            out_ref[base + TOK : base + TOK + 16, :] = block[:, HD:]


def pick_kernel(wanted, zg_ref, out_ref):
    for d in range(NY):
        for z in range(NZ):
            out_ref[d, z * 2 * W_ROWS : (z + 1) * 2 * W_ROWS, :] = zg_ref[z, : 2 * W_ROWS, :]
        for i in range(SLOTS):
            p = wanted[d, i] & 7
            src = pl.ds(pl.multiple_of(2 * W_ROWS + (p & 1) * C_ROWS, 64), C_ROWS)
            base = NZ * 2 * W_ROWS + i * C_ROWS
            out_ref[d, base : base + C_ROWS, :] = zg_ref[p >> 1, src, :]


def project(place, core, mine, from_ref, h_refs, bias_ref, cos_ref, sin_ref, wt_ref, put):
    for y in range(NY):
        for z in range(NZ):
            for half in range(2):
                lo = ((y * NZ + z) * 2 + half) * 128
                wt_ref[:, lo : lo + 128] = from_ref[
                    y, (z * 2 + half) * W_ROWS : (z * 2 + half + 1) * W_ROWS, :
                ]
    at = pl.ds(pl.multiple_of(place[0] * 16 + core * 8, 8), 8)
    cosine = cos_ref[at, :]
    sine = sin_ref[at, :]
    bias = bias_ref[core]
    for h_ref, shift in zip(h_refs, (0, 3, 1, 2)):
        mixed = lax.dot_general(
            wt_ref[...], h_ref[...], (((1,), (1,)), ((), ())), preferred_element_type=jnp.float32
        )
        mixed = mixed + bias
        to = (place[0] + shift) & 3
        for g in range(HEADS):
            lo = mixed[g * 16 : g * 16 + 8]
            hi = mixed[g * 16 + 8 : g * 16 + 16]
            if g < GROUP + 1:
                lo, hi = lo * cosine - hi * sine, hi * cosine + lo * sine
            both = jnp.concatenate([lo, hi], axis=0).astype(jnp.bfloat16)
            put(to, slice(g * 16, g * 16 + 16), both)
    for i in range(SLOTS):
        base = NZ * 2 * W_ROWS + i * C_ROWS
        rows = from_ref[mine[i] >> 3, base : base + C_ROWS, :]
        to = W_ROWS + i * C_ROWS
        for d in range(NX):
            put(d, slice(to, to + C_ROWS), rows)


def first_kernel(
    place, mine, a_ref, h0, h1, h2, h3, bias_ref, cos_ref, sin_ref, out_ref, wt_ref
):
    def put(d, rows, value):
        out_ref[d, rows, :] = value

    hs = (h0, h1, h2, h3)
    project(place, place[1], mine, a_ref, hs, bias_ref, cos_ref, sin_ref, wt_ref, put)


def second_kernel(
    place, mine, b_ref, h0, h1, h2, h3, bias_ref, cos_ref, sin_ref, part_ref, out_ref, wt_ref
):
    c = place[1]

    def put(d, rows, value):
        out_ref[d, 1 - c, rows, :] = value

    hs = (h0, h1, h2, h3)
    project(place, 1 - c, mine, b_ref, hs, bias_ref, cos_ref, sin_ref, wt_ref, put)
    for d in range(NX):
        out_ref[d, c] = part_ref[d]


def attend_kernel(g_ref, live_ref, out_ref, q_ref, kn_ref, vn_ref, kc_ref, vc_ref):
    for x in range(NX):
        for g in range(HEADS):
            pair = [g_ref[x, c, g * 16 : g * 16 + 16, :].astype(jnp.float32) for c in range(NC)]
            for half in range(2):
                rows = jnp.concatenate([p[half * 8 : half * 8 + 8] for p in pair], axis=0)
                rows = rows.astype(jnp.bfloat16)
                at = slice(half * 64 + x * 16, half * 64 + x * 16 + 16)
                if g < GROUP:
                    q_ref[at, g * 128 : (g + 1) * 128] = rows
                elif g == GROUP:
                    kn_ref[at, :] = rows
                else:
                    vn_ref[at, :] = rows
        for k in range(NC):
            for i in range(SLOTS):
                base = W_ROWS + i * C_ROWS
                at = slice((x * NC + k) * TOK, (x * NC + k + 1) * TOK)
                kc_ref[i, at, :] = g_ref[x, k, base : base + TOK, :]
                vc_ref[i, at, :] = g_ref[x, k, base + TOK : base + 2 * TOK, :]
    q = q_ref[...]
    scaling = HD ** (-0.5)
    lane = lax.broadcasted_iota(jnp.int32, (1, GROUP * ROWS), 1) & (ROWS - 1)
    second = lane >= ROWS // 2

    def plain(a, b):
        return jnp.dot(a, b, preferred_element_type=jnp.float32)

    def turned(a, b):
        return lax.dot_general(a, b, (((0,), (0,)), ((), ())), preferred_element_type=jnp.float32)

    scores = jnp.where(second, plain(kc_ref[1], q), plain(kc_ref[0], q)) * scaling
    own = turned(kn_ref[...], q) * scaling
    token = lax.broadcasted_iota(jnp.int32, (ROWS, GROUP * ROWS), 0)
    seen = ((token >> 2) == (lane >> 2)) & ((token & 3) <= (lane & 3))
    own = jnp.where(seen, own, -jnp.inf)
    row_max = jnp.maximum(
        jnp.max(scores, axis=0, keepdims=True), jnp.max(own, axis=0, keepdims=True)
    )
    prompt_exp = jnp.exp(scores - row_max)
    own_exp = jnp.exp(own - row_max)
    total = jnp.sum(prompt_exp, axis=0, keepdims=True) + jnp.sum(own_exp, axis=0, keepdims=True)
    weights = prompt_exp.astype(jnp.bfloat16)
    out = jnp.where(second, turned(vc_ref[1], weights), turned(vc_ref[0], weights))
    out = out + plain(vn_ref[...], own_exp.astype(jnp.bfloat16))
    out = out / total
    for h in range(GROUP):
        part = out[:, h * 128 : (h + 1) * 128]
        part = jnp.where(live_ref[...] > 0, part, 0.0)
        out_ref[:, h * 128 : (h + 1) * 128] = part.T.astype(jnp.bfloat16)


def tables():
    inverse = 1000000.0 ** (-2.0 * np.arange(64) / HD)
    step = np.arange(ROWS) % STEPS
    angles = (PLEN + step)[None, :] * inverse[:, None]
    return np.cos(angles).astype(np.float32), np.sin(angles).astype(np.float32)


def call(kernel, shape, specs, dtype=jnp.bfloat16, scratch=(), flops=0, moved=0, limit=8):
    return pl.pallas_call(
        kernel,
        out_shape=jax.ShapeDtypeStruct(shape, dtype),
        in_specs=specs,
        out_specs=vmem(),
        scratch_shapes=list(scratch),
        cost_estimate=pl.CostEstimate(flops=flops, bytes_accessed=moved, transcendentals=0),
        compiler_params=pltpu.CompilerParams(vmem_limit_bytes=limit * 2**20),
        interpret=INTERPRET,
    )


def hop(array, axis, size, by):
    return lax.ppermute(array, axis, [(i, (i + by) % size) for i in range(size)])


def step(hidden, qkv_weight, qkv_bias, prompt_pool, block_table, group_prompts, decode_len):
    bf16 = jnp.bfloat16
    x = lax.axis_index("x").astype(jnp.int32)
    c = lax.axis_index("c").astype(jnp.int32)
    place = jnp.stack([x, c])

    h0 = hidden.reshape(ROWS, WIDTH)
    h1 = hop(h0, "x", NX, 1)
    h2 = hop(h0, "x", NX, -1)
    h3 = hop(h0, "x", NX, 2)
    wanted = jnp.broadcast_to(group_prompts[None], (NY, SLOTS))
    wanted = lax.all_to_all(wanted, "y", 0, 0, tiled=True)

    sent = call(
        prep_kernel, (Z_ROWS, 128), [smem(), smem(), vmem(), vmem()], moved=600000
    )(
        place,
        block_table,
        qkv_weight.reshape(K_SHARD, HEADS * HD),
        prompt_pool.reshape(SLOTS, 6, 16, 2 * HD),
    )
    zg = lax.all_gather(sent, "zh", axis=0, tiled=True)
    zg = zg.reshape(NZ, Z_ROWS, 128)
    picked = call(pick_kernel, (NY, Y_ROWS, 128), [smem(), vmem()], moved=1500000)(wanted, zg)
    a = lax.all_to_all(picked, "y", 0, 0, tiled=True)
    b = hop(a, "c", NC, 1)

    bias = lax.dynamic_index_in_dim(
        qkv_bias.reshape(HEADS * 2, NX, NC, 8), x, 1, keepdims=False
    )
    bias = bias.transpose(1, 0, 2).reshape(NC, W_ROWS, 1)
    bias = jnp.broadcast_to(bias, (NC, W_ROWS, ROWS))
    cosine, sine = tables()
    cosine, sine = jnp.asarray(cosine), jnp.asarray(sine)
    scratch = [pltpu.VMEM((W_ROWS, WIDTH), bf16)]
    flops = 2 * W_ROWS * WIDTH * 4 * ROWS
    part = call(
        first_kernel,
        (NX, X_ROWS, 128),
        [smem(), smem()] + [vmem()] * 8,
        scratch=scratch,
        flops=flops,
        moved=5500000,
        limit=16,
    )(place, group_prompts, a, h0, h1, h2, h3, bias, cosine, sine)
    made = call(
        second_kernel,
        (NX, NC, X_ROWS, 128),
        [smem(), smem()] + [vmem()] * 9,
        scratch=scratch,
        flops=flops,
        moved=6500000,
        limit=16,
    )(place, group_prompts, b, h0, h1, h2, h3, bias, cosine, sine, part)
    got = lax.all_to_all(made, "x", 0, 0, tiled=True)

    step = jnp.arange(STEPS, dtype=jnp.int32)
    live = (step[None, None, :] < decode_len[:, :, None]).astype(jnp.float32).reshape(1, ROWS)
    out = call(
        attend_kernel,
        (ROWS, GROUP * HD),
        [vmem(), vmem()],
        scratch=[
            pltpu.VMEM((HD, GROUP * ROWS), bf16),
            pltpu.VMEM((HD, ROWS), bf16),
            pltpu.VMEM((HD, ROWS), bf16),
            pltpu.VMEM((SLOTS, PLEN, HD), bf16),
            pltpu.VMEM((SLOTS, PLEN, HD), bf16),
        ],
        flops=400000000,
        moved=1000000,
        limit=16,
    )(got, live)
    return out.reshape(SLOTS, SAMPLES_DEV, STEPS, 1, GROUP * HD)


def solution(mesh):
    names = ("y", "zh", "x", "c", "tp")
    fine = Mesh(mesh.devices.reshape(NY, NZ, NX, NC, mesh.shape["tp"]), names)
    fsdp, sample = ("y", "zh"), ("x", "c")
    return jax.shard_map(
        step,
        mesh=fine,
        in_specs=(
            P(fsdp, sample, None, None),
            P(fsdp, "tp", None),
            P("tp", None),
            P(fsdp, sample, None, "tp", None),
            P(fsdp, sample),
            P(fsdp),
            P(fsdp, sample),
        ),
        out_specs=P(fsdp, sample, None, "tp", None),
        check_vma=False,
    )
```

profile of v0, /device:TPU:8, one launch (start us, length us, event | category | flops | bytes accessed | tf_op | source)
XLA Modules:
  0.0 148.5 jit_solution(17820160830298461092)
XLA Ops:
  0.0 1.2 broadcast_in_dim.6
  1.2 16.3 %all-to-all-start = ((s32[4,1,2]{2,1,0:T(1,128)}), s32[4,1,2]{2,1,0:T(1,128)S(1)}, u32[]{:S(2)}, u32[]{:S(2)}) async-start(s32[4,1,2]{2,1,0:T(1,128)} %broadcast_in_dim.6), calls=%async_computation | async-start | bytes 4096 | tf_op jit(solution)/shard_map/all_to_all | solution.py:214
  17.6 0.7 copy-done.5
  18.3 1.0 copy-done
  19.2 0.9 copy-done.3
  20.1 0.8 shard_map.91
  20.9 50.3 %all_gather.3 = bf16[1792,128]{1,0:T(8,128)(2,1)S(1)} all-gather(bf16[448,128]{1,0:T(8,128)(2,1)S(1)} %shard_map.91), channel_id=1, replica_groups=mesh['y'=4,'zh'=4,'x'=4,'c'=2,'tp'=8] {'zh'}, dimensions={0}, use_global_device_ids=true | all-gather | bytes 573440 | tf_op jit(solution)/shard_map/all_gather | solution.py:224
  71.2 1.7 %shard_map.92 = bf16[4,1024,128]{2,1,0:T(8,128)(2,1)} custom-call(s32[4,2]{1,0:T(4,128)S(1)} %bitcast.15, bf16[4,448,128]{2,1,0:T(8,128)(2,1)S(1)} %bitcast.12), custom_call_target="tpu_custom_call" | custom-call | bytes 1500000 | tf_op jit(solution)/shard_map/pallas_call | solution.py:226
  72.9 4.9 %all-to-all-start.1 = ((bf16[4,1024,128]{2,1,0:T(8,128)(2,1)}), bf16[4,1024,128]{2,1,0:T(8,128)(2,1)S(1)}, u32[]{:S(2)}, u32[]{:S(2)}) async-start(bf16[4,1024,128]{2,1,0:T(8,128)(2,1)} %shard_map.92), calls=%async_computation.1 | async-start | bytes 2097152 | tf_op jit(solution)/shard_map/all_to_all | solution.py:227
  77.8 0.3 reshape.58.h0
  78.1 3.3 %collective-permute-start.1 = (bf16[128,4096]{1,0:T(8,128)(2,1)S(1)}, bf16[128,4096]{1,0:T(8,128)(2,1)S(1)}, u32[]{:S(2)}, u32[]{:S(2)}) collective-permute-start(bf16[128,4096]{1,0:T(8,128)(2,1)S(1)} %reshape.58.h0), channel_id=1, source_target_pairs={{0,16},{16,32},{32,48},{48,0},{1,17},{17,33},{33,49},{49,1},{2,18}... | collective-permute-start | bytes 3145736 | tf_op jit(solution)/shard_map/ppermute | solution.py:200
  81.4 3.7 %collective-permute-start.2 = (bf16[128,4096]{1,0:T(8,128)(2,1)S(1)}, bf16[128,4096]{1,0:T(8,128)(2,1)}, u32[]{:S(2)}, u32[]{:S(2)}) collective-permute-start(bf16[128,4096]{1,0:T(8,128)(2,1)S(1)} %reshape.58.h0), channel_id=1, source_target_pairs={{0,48},{16,0},{32,16},{48,32},{1,49},{17,1},{33,17},{49,33},{2,50}... | collective-permute-start | bytes 3145736 | tf_op jit(solution)/shard_map/ppermute | solution.py:200
  85.1 3.7 %collective-permute-start.3 = (bf16[128,4096]{1,0:T(8,128)(2,1)S(1)}, bf16[128,4096]{1,0:T(8,128)(2,1)}, u32[]{:S(2)}, u32[]{:S(2)}) collective-permute-start(bf16[128,4096]{1,0:T(8,128)(2,1)S(1)} %reshape.58.h0), channel_id=1, source_target_pairs={{0,32},{16,48},{32,0},{48,16},{1,33},{17,49},{33,1},{49,17},{2,34}... | collective-permute-start | bytes 3145736 | tf_op jit(solution)/shard_map/ppermute | solution.py:200
  88.8 1.9 %collective-permute-start = (bf16[4,1024,128]{2,1,0:T(8,128)(2,1)S(1)}, bf16[4,1024,128]{2,1,0:T(8,128)(2,1)}, u32[]{:S(2)}, u32[]{:S(2)}) collective-permute-start(bf16[4,1024,128]{2,1,0:T(8,128)(2,1)S(1)} %all-to-all-done.1.a_ref), channel_id=1, source_target_pairs={{0,8},{8,0},{1,9},{9,1},{2,10},{10,2},{3,11},{11,3},{4,12},{12,4},... | collective-permute-start | bytes 3145736 | tf_op jit(solution)/shard_map/ppermute | solution.py:200
  90.8 0.1 reshape.59
  91.1 14.8 %collective-permute-done.1.h1 = bf16[128,4096]{1,0:T(8,128)(2,1)S(1)} collective-permute-done((bf16[128,4096]{1,0:T(8,128)(2,1)S(1)}, bf16[128,4096]{1,0:T(8,128)(2,1)S(1)}, u32[]{:S(2)}, u32[]{:S(2)}) %collective-permute-start.1) | collective-permute-done | bytes 1048608 | tf_op jit(solution)/shard_map/ppermute | solution.py:200
  105.9 3.6 %collective-permute-done.2.h2 = bf16[128,4096]{1,0:T(8,128)(2,1)} collective-permute-done((bf16[128,4096]{1,0:T(8,128)(2,1)S(1)}, bf16[128,4096]{1,0:T(8,128)(2,1)}, u32[]{:S(2)}, u32[]{:S(2)}) %collective-permute-start.2) | collective-permute-done | bytes 1048608 | tf_op jit(solution)/shard_map/ppermute | solution.py:200
  109.4 15.5 %collective-permute-done.3.h3 = bf16[128,4096]{1,0:T(8,128)(2,1)} collective-permute-done((bf16[128,4096]{1,0:T(8,128)(2,1)S(1)}, bf16[128,4096]{1,0:T(8,128)(2,1)}, u32[]{:S(2)}, u32[]{:S(2)}) %collective-permute-start.3) | collective-permute-done | bytes 1048608 | tf_op jit(solution)/shard_map/ppermute | solution.py:200
  125.1 3.0 %shard_map.93.part_ref = bf16[4,352,128]{2,1,0:T(8,128)(2,1)S(1)} custom-call(s32[2]{0:T(128)S(1)} %pad_add_fusion.place, s32[2]{0:T(128)S(1)} %copy-done.4, bf16[4,1024,128]{2,1,0:T(8,128)(2,1)S(1)} %all-to-all-done.1.a_ref, bf16[128,4096]{1,0:T(8,128)(2,1)S(1)} %reshape.58.h0, bf16[128,4096]{1,0:T(8,128)(2,1)S(1)} %collective-permute-done.1.h1, ...), custom_call_target="tpu_custom_call" | custom-call | flops 402653184 | bytes 5500000 | tf_op jit(solution)/shard_map/pallas_call | solution.py:239
  128.1 4.3 %shard_map.94 = bf16[4,2,352,128]{3,2,1,0:T(8,128)(2,1)} custom-call(s32[2]{0:T(128)S(1)} %pad_add_fusion.place, s32[2]{0:T(128)S(1)} %copy-done.4, bf16[4,1024,128]{2,1,0:T(8,128)(2,1)} %collective-permute-done.b_ref, bf16[128,4096]{1,0:T(8,128)(2,1)S(1)} %reshape.58.h0, bf16[128,4096]{1,0:T(8,128)(2,1)S(1)} %collective-permute-done.1.h1, ...), custom_call_target="tpu_custom_call" | custom-call | flops 402653184 | bytes 6500000 | tf_op jit(solution)/shard_map/pallas_call | solution.py:248
  132.4 5.1 %all-to-all-start.2 = ((bf16[4,2,352,128]{3,2,1,0:T(8,128)(2,1)}), bf16[4,2,352,128]{3,2,1,0:T(8,128)(2,1)S(1)}, u32[]{:S(2)}, u32[]{:S(2)}) async-start(bf16[4,2,352,128]{3,2,1,0:T(8,128)(2,1)} %shard_map.94), calls=%async_computation.2 | async-start | bytes 1441792 | tf_op jit(solution)/shard_map/all_to_all | solution.py:257
  137.7 9.0 %all-to-all-done.2.g_ref = bf16[4,2,352,128]{3,2,1,0:T(8,128)(2,1)S(1)} async-done(((bf16[4,2,352,128]{3,2,1,0:T(8,128)(2,1)}), bf16[4,2,352,128]{3,2,1,0:T(8,128)(2,1)S(1)}, u32[]{:S(2)}, u32[]{:S(2)}) %all-to-all-start.2) | async-done | bytes 720928 | tf_op jit(solution)/shard_map/all_to_all | solution.py:257
  146.7 1.1 shard_map.95
  147.8 0.7 reshape.60
  (26 shorter events, 0.5 us)
Async XLA Ops:
  1.2 70.0 %all-to-all-start = ((s32[4,1,2]{2,1,0:T(1,128)}), s32[4,1,2]{2,1,0:T(1,128)S(1)}, u32[]{:S(2)}, u32[]{:S(2)}) async-start(s32[4,1,2]{2,1,0:T(1,128)} %broadcast_in_dim.6), calls=%async_computation | async-start | bytes 4096 | tf_op jit(solution)/shard_map/all_to_all | solution.py:214
  17.6 0.7 copy-start.5
  18.2 1.0 copy-start
  19.2 0.9 copy-start.3
  72.9 4.9 %copy-start.6 = (bf16[2,16,4,4096]{3,2,1,0:T(4,128)(2,1)S(1)}, bf16[2,16,4,4096]{3,2,1,0:T(4,128)(2,1)}, u32[]{:S(2)}) copy-start(bf16[2,16,4,4096]{3,2,1,0:T(4,128)(2,1)} %param.9) | copy-start | bytes 3145732
  72.9 16.0 %all-to-all-start.1 = ((bf16[4,1024,128]{2,1,0:T(8,128)(2,1)}), bf16[4,1024,128]{2,1,0:T(8,128)(2,1)S(1)}, u32[]{:S(2)}, u32[]{:S(2)}) async-start(bf16[4,1024,128]{2,1,0:T(8,128)(2,1)} %shard_map.92), calls=%async_computation.1 | async-start | bytes 2097152 | tf_op jit(solution)/shard_map/all_to_all | solution.py:227
  77.8 13.0 %copy-start.7 = (f32[1,768]{1,0:T(1,128)S(1)}, f32[1,768]{1,0:T(1,128)}, u32[]{:S(2)}) copy-start(f32[1,768]{1,0:T(1,128)} %param.11) | copy-start | bytes 9220
  78.1 27.8 %collective-permute-start.1 = (bf16[128,4096]{1,0:T(8,128)(2,1)S(1)}, bf16[128,4096]{1,0:T(8,128)(2,1)S(1)}, u32[]{:S(2)}, u32[]{:S(2)}) collective-permute-start(bf16[128,4096]{1,0:T(8,128)(2,1)S(1)} %reshape.58.h0), channel_id=1, source_target_pairs={{0,16},{16,32},{32,48},{48,0},{1,17},{17,33},{33,49},{49,1},{2,18}... | collective-permute-start | bytes 3145736 | tf_op jit(solution)/shard_map/ppermute | solution.py:200
  81.4 28.0 %collective-permute-start.2 = (bf16[128,4096]{1,0:T(8,128)(2,1)S(1)}, bf16[128,4096]{1,0:T(8,128)(2,1)}, u32[]{:S(2)}, u32[]{:S(2)}) collective-permute-start(bf16[128,4096]{1,0:T(8,128)(2,1)S(1)} %reshape.58.h0), channel_id=1, source_target_pairs={{0,48},{16,0},{32,16},{48,32},{1,49},{17,1},{33,17},{49,33},{2,50}... | collective-permute-start | bytes 3145736 | tf_op jit(solution)/shard_map/ppermute | solution.py:200
  85.1 39.9 %collective-permute-start.3 = (bf16[128,4096]{1,0:T(8,128)(2,1)S(1)}, bf16[128,4096]{1,0:T(8,128)(2,1)}, u32[]{:S(2)}, u32[]{:S(2)}) collective-permute-start(bf16[128,4096]{1,0:T(8,128)(2,1)S(1)} %reshape.58.h0), channel_id=1, source_target_pairs={{0,32},{16,48},{32,0},{48,16},{1,33},{17,49},{33,1},{49,17},{2,34}... | collective-permute-start | bytes 3145736 | tf_op jit(solution)/shard_map/ppermute | solution.py:200
  88.8 39.3 %collective-permute-start = (bf16[4,1024,128]{2,1,0:T(8,128)(2,1)S(1)}, bf16[4,1024,128]{2,1,0:T(8,128)(2,1)}, u32[]{:S(2)}, u32[]{:S(2)}) collective-permute-start(bf16[4,1024,128]{2,1,0:T(8,128)(2,1)S(1)} %all-to-all-done.1.a_ref), channel_id=1, source_target_pairs={{0,8},{8,0},{1,9},{9,1},{2,10},{10,2},{3,11},{11,3},{4,12},{12,4},... | collective-permute-start | bytes 3145736 | tf_op jit(solution)/shard_map/ppermute | solution.py:200
  91.0 34.0 %copy-start.1 = (f32[64,128]{1,0:T(8,128)S(1)}, f32[64,128]{1,0:T(8,128)}, u32[]{:S(2)}) copy-start(f32[64,128]{1,0:T(8,128)} %constant.21.clone.cos_ref) | copy-start | bytes 98308
  91.0 34.0 %copy-start.2 = (f32[64,128]{1,0:T(8,128)S(1)}, f32[64,128]{1,0:T(8,128)}, u32[]{:S(2)}) copy-start(f32[64,128]{1,0:T(8,128)} %constant.22.clone.sin_ref) | copy-start | bytes 98308
  91.0 34.0 %copy-start.4 = (s32[2]{0:T(128)S(1)}, s32[2]{0:T(128)}, u32[]{:S(2)}) copy-start(s32[2]{0:T(128)} %mine.3) | copy-start | bytes 28
  132.4 5.1 %copy-start.8 = (s32[2,16]{1,0:T(2,128)S(1)}, s32[2,16]{1,0:T(2,128)}, u32[]{:S(2)}) copy-start(s32[2,16]{1,0:T(2,128)} %param.15) | copy-start | bytes 388
  132.4 14.3 %all-to-all-start.2 = ((bf16[4,2,352,128]{3,2,1,0:T(8,128)(2,1)}), bf16[4,2,352,128]{3,2,1,0:T(8,128)(2,1)S(1)}, u32[]{:S(2)}, u32[]{:S(2)}) async-start(bf16[4,2,352,128]{3,2,1,0:T(8,128)(2,1)} %shard_map.94), calls=%async_computation.2 | async-start | bytes 1441792 | tf_op jit(solution)/shard_map/all_to_all | solution.py:257
where the time goes:
time: 149 us
  blocking collectives  50.3 us (34%)
  waiting for transfers between devices  42.9 us (29%)
  starting transfers between devices  39 us (26%)
  Pallas kernels  10.8 us (7%)
  local copies, waits for them, and re-layouts  5.19 us (3%)
    all_gather x1, blocking collectives, step(): zg = lax.all_gather(sent, 'zh', axis=0, tiled=True)  50.3 us
    ppermute x4, waiting for transfers between devices, hop(): lax.ppermute(array, axis, [(i, (i + by) % size) for i in range(size)])  33.9 us
    all_to_all x1, starting transfers between devices, step(): wanted = lax.all_to_all(wanted, 'y', 0, 0, tiled=True)  16.3 us
    ppermute x4, starting transfers between devices, hop(): lax.ppermute(array, axis, [(i, (i + by) % size) for i in range(size)])  12.6 us
    all_to_all x1, waiting for transfers between devices, step(): got = lax.all_to_all(made, 'x', 0, 0, tiled=True)  8.95 us
    all_to_all x1, starting transfers between devices, step(): got = lax.all_to_all(made, 'x', 0, 0, tiled=True)  5.14 us
    all_to_all x1, starting transfers between devices, step(): a = lax.all_to_all(picked, 'y', 0, 0, tiled=True)  4.93 us
    pallas_call x1, Pallas kernels, step(): call(second_kernel, (NX, NC, X_ROWS, 128), [smem(), smem()] + [vmem()] *...  4.29 us
  transfers between devices with their start and end apart: 7, of which 4 were waited for; matrix products, arithmetic and copies ran while one was open for 1% of the time, Pallas kernels for 3%

commit v1 on v0

--- a/solution.py
+++ b/solution.py
@@ -44,7 +44,7 @@
             for g in range(HEADS * 2):
                 lo = g * 64 + k * 8
                 for half in range(2):
-                    out_ref[half * W_ROWS + g * 8 : half * W_ROWS + (g + 1) * 8, :] = wt[
+                    out_ref[0, half * W_ROWS + g * 8 : half * W_ROWS + (g + 1) * 8, :] = wt[
                         lo : lo + 8, half * 128 : (half + 1) * 128
                     ]
 
@@ -52,16 +52,19 @@
         for b in range(4):
             block = pool_ref[i, table[i, b]]
             base = 2 * W_ROWS + i * C_ROWS + b * 16
-            out_ref[base : base + 16, :] = block[:, :HD]
-            out_ref[base + TOK : base + TOK + 16, :] = block[:, HD:]
-
-
-def pick_kernel(wanted, zg_ref, out_ref):
-    for d in range(NY):
+            out_ref[0, base : base + 16, :] = block[:, :HD]
+            out_ref[0, base + TOK : base + TOK + 16, :] = block[:, HD:]
+    for d in range(1, NZ):
+        out_ref[d] = out_ref[0]
+
+
+def pick_kernel(place, w0, w1, w2, w3, zg_ref, out_ref):
+    for back, wanted in enumerate((w0, w1, w2, w3)):
+        d = (place[2] - back) & 3
         for z in range(NZ):
             out_ref[d, z * 2 * W_ROWS : (z + 1) * 2 * W_ROWS, :] = zg_ref[z, : 2 * W_ROWS, :]
         for i in range(SLOTS):
-            p = wanted[d, i] & 7
+            p = wanted[i] & 7
             src = pl.ds(pl.multiple_of(2 * W_ROWS + (p & 1) * C_ROWS, 64), C_ROWS)
             base = NZ * 2 * W_ROWS + i * C_ROWS
             out_ref[d, base : base + C_ROWS, :] = zg_ref[p >> 1, src, :]
@@ -204,26 +207,29 @@
     bf16 = jnp.bfloat16
     x = lax.axis_index("x").astype(jnp.int32)
     c = lax.axis_index("c").astype(jnp.int32)
-    place = jnp.stack([x, c])
+    y = lax.axis_index("y").astype(jnp.int32)
+    place = jnp.stack([x, c, y])
 
     h0 = hidden.reshape(ROWS, WIDTH)
     h1 = hop(h0, "x", NX, 1)
     h2 = hop(h0, "x", NX, -1)
     h3 = hop(h0, "x", NX, 2)
-    wanted = jnp.broadcast_to(group_prompts[None], (NY, SLOTS))
-    wanted = lax.all_to_all(wanted, "y", 0, 0, tiled=True)
+    wanted = [group_prompts]
+    for by in range(1, NY):
+        wanted.append(hop(group_prompts, "y", NY, by))
 
     sent = call(
-        prep_kernel, (Z_ROWS, 128), [smem(), smem(), vmem(), vmem()], moved=600000
+        prep_kernel, (NZ, Z_ROWS, 128), [smem(), smem(), vmem(), vmem()], moved=600000
     )(
         place,
         block_table,
         qkv_weight.reshape(K_SHARD, HEADS * HD),
         prompt_pool.reshape(SLOTS, 6, 16, 2 * HD),
     )
-    zg = lax.all_gather(sent, "zh", axis=0, tiled=True)
-    zg = zg.reshape(NZ, Z_ROWS, 128)
-    picked = call(pick_kernel, (NY, Y_ROWS, 128), [smem(), vmem()], moved=1500000)(wanted, zg)
+    zg = lax.all_to_all(sent, "zh", 0, 0, tiled=True)
+    picked = call(pick_kernel, (NY, Y_ROWS, 128), [smem()] * 5 + [vmem()], moved=1500000)(
+        place, *wanted, zg
+    )
     a = lax.all_to_all(picked, "y", 0, 0, tiled=True)
     b = hop(a, "c", NC, 1)
 

time: 149 us -> 168 us (1.13)
  the two profiles are of different devices: /device:TPU:8 before, /device:TPU:40 now
where the time goes in v1:
time: 168 us; the launch traced here: 167 us
  waiting for transfers between devices  90.4 us (54%)
  starting transfers between devices  61.1 us (36%)
  Pallas kernels  11.7 us (7%)
  local copies, waits for them, and re-layouts  3.96 us (2%)
    all_to_all x1, waiting for transfers between devices, step(): zg = lax.all_to_all(sent, 'zh', 0, 0, tiled=True)  45.5 us
    ppermute x7, waiting for transfers between devices, hop(): lax.ppermute(array, axis, [(i, (i + by) % size) for i in range(size)])  36 us
    all_to_all x1, starting transfers between devices, step(): zg = lax.all_to_all(sent, 'zh', 0, 0, tiled=True)  27.6 us
    ppermute x7, starting transfers between devices, hop(): lax.ppermute(array, axis, [(i, (i + by) % size) for i in range(size)])  23.3 us
    all_to_all x1, waiting for transfers between devices, step(): got = lax.all_to_all(made, 'x', 0, 0, tiled=True)  8.95 us
    all_to_all x1, starting transfers between devices, step(): got = lax.all_to_all(made, 'x', 0, 0, tiled=True)  5.18 us
    all_to_all x1, starting transfers between devices, step(): a = lax.all_to_all(picked, 'y', 0, 0, tiled=True)  5.04 us
    pallas_call x1, Pallas kernels, step(): call(second_kernel, (NX, NC, X_ROWS, 128), [smem(), smem()] + [vmem()] *...  4.28 us
  transfers between devices with their start and end apart: 10, of which 5 were waited for; matrix products, arithmetic and copies ran while one was open for 0% of the time, Pallas kernels for 2%

profile of v1, /device:TPU:40, one launch (start us, length us, event | category | flops | bytes accessed | tf_op | source)
XLA Modules:
  0.0 167.5 jit_solution(11279827725888134013)
XLA Ops:
  0.1 0.7 copy-done.5
  0.8 1.0 copy-done
  1.8 0.9 copy-done.3
  2.6 1.6 shard_map.91
  4.2 27.6 %all-to-all-start = ((bf16[4,448,128]{2,1,0:T(8,128)(2,1)}), bf16[4,448,128]{2,1,0:T(8,128)(2,1)S(1)}, u32[]{:S(2)}, u32[]{:S(2)}) async-start(bf16[4,448,128]{2,1,0:T(8,128)(2,1)} %shard_map.91), calls=%async_computation | async-start | bytes 917504 | tf_op jit(solution)/shard_map/all_to_all | solution.py:229
  31.8 3.5 %collective-permute-start = (s32[2]{0:T(128)S(1)}, s32[2]{0:T(128)S(1)}, u32[]{:S(2)}, u32[]{:S(2)}) collective-permute-start(s32[2]{0:T(128)S(1)} %copy-done.4), channel_id=1, source_target_pairs={{0,256},{256,512},{512,768},{768,0},{1,257},{257,513},{513,769},{7... | collective-permute-start | bytes 32 | tf_op jit(solution)/shard_map/ppermute | solution.py:203
  35.3 2.8 %collective-permute-start.1 = (s32[2]{0:T(128)S(1)}, s32[2]{0:T(128)S(1)}, u32[]{:S(2)}, u32[]{:S(2)}) collective-permute-start(s32[2]{0:T(128)S(1)} %copy-done.4), channel_id=1, source_target_pairs={{0,512},{256,768},{512,0},{768,256},{1,513},{257,769},{513,1},{769... | collective-permute-start | bytes 32 | tf_op jit(solution)/shard_map/ppermute | solution.py:203
  38.1 4.3 %collective-permute-start.2 = (s32[2]{0:T(128)S(1)}, s32[2]{0:T(128)S(1)}, u32[]{:S(2)}, u32[]{:S(2)}) collective-permute-start(s32[2]{0:T(128)S(1)} %copy-done.4), channel_id=1, source_target_pairs={{0,768},{256,0},{512,256},{768,512},{1,769},{257,1},{513,257},{769... | collective-permute-start | bytes 32 | tf_op jit(solution)/shard_map/ppermute | solution.py:203
  42.5 1.3 collective-permute-done.2.w3
  43.7 45.5 %all-to-all-done.zg_ref = bf16[4,448,128]{2,1,0:T(8,128)(2,1)S(1)} async-done(((bf16[4,448,128]{2,1,0:T(8,128)(2,1)}), bf16[4,448,128]{2,1,0:T(8,128)(2,1)S(1)}, u32[]{:S(2)}, u32[]{:S(2)}) %all-to-all-start) | async-done | bytes 458784 | tf_op jit(solution)/shard_map/all_to_all | solution.py:229
  89.2 1.7 %shard_map.92 = bf16[4,1024,128]{2,1,0:T(8,128)(2,1)} custom-call(s32[3]{0:T(128)S(1)} %pad_add_fusion.place, s32[2]{0:T(128)S(1)} %copy-done.4, s32[2]{0:T(128)S(1)} %collective-permute-done.w1, s32[2]{0:T(128)S(1)} %collective-permute-done.1.w2, s32[2]{0:T(128)S(1)} %collective-permute-done.2.w3, bf16[4,448,128]{2,1,0:T(8,128)(2,1)S(1)} %all-to-all-done.zg_ref), custom_call_target="tpu_custom_call" | custom-call | bytes 1500000 | tf_op jit(solution)/shard_map/pallas_call | solution.py:230
  90.9 5.0 %all-to-all-start.1 = ((bf16[4,1024,128]{2,1,0:T(8,128)(2,1)}), bf16[4,1024,128]{2,1,0:T(8,128)(2,1)S(1)}, u32[]{:S(2)}, u32[]{:S(2)}) async-start(bf16[4,1024,128]{2,1,0:T(8,128)(2,1)} %shard_map.92), calls=%async_computation.1 | async-start | bytes 2097152 | tf_op jit(solution)/shard_map/all_to_all | solution.py:233
  96.2 3.4 %collective-permute-start.4 = (bf16[128,4096]{1,0:T(8,128)(2,1)S(1)}, bf16[128,4096]{1,0:T(8,128)(2,1)S(1)}, u32[]{:S(2)}, u32[]{:S(2)}) collective-permute-start(bf16[128,4096]{1,0:T(8,128)(2,1)S(1)} %reshape.48.h0), channel_id=1, source_target_pairs={{0,16},{16,32},{32,48},{48,0},{1,17},{17,33},{33,49},{49,1},{2,18}... | collective-permute-start | bytes 3145736 | tf_op jit(solution)/shard_map/ppermute | solution.py:203
  99.6 3.7 %collective-permute-start.5 = (bf16[128,4096]{1,0:T(8,128)(2,1)S(1)}, bf16[128,4096]{1,0:T(8,128)(2,1)}, u32[]{:S(2)}, u32[]{:S(2)}) collective-permute-start(bf16[128,4096]{1,0:T(8,128)(2,1)S(1)} %reshape.48.h0), channel_id=1, source_target_pairs={{0,48},{16,0},{32,16},{48,32},{1,49},{17,1},{33,17},{49,33},{2,50}... | collective-permute-start | bytes 3145736 | tf_op jit(solution)/shard_map/ppermute | solution.py:203
  103.3 3.7 %collective-permute-start.6 = (bf16[128,4096]{1,0:T(8,128)(2,1)S(1)}, bf16[128,4096]{1,0:T(8,128)(2,1)}, u32[]{:S(2)}, u32[]{:S(2)}) collective-permute-start(bf16[128,4096]{1,0:T(8,128)(2,1)S(1)} %reshape.48.h0), channel_id=1, source_target_pairs={{0,32},{16,48},{32,0},{48,16},{1,33},{17,49},{33,1},{49,17},{2,34}... | collective-permute-start | bytes 3145736 | tf_op jit(solution)/shard_map/ppermute | solution.py:203
  107.0 1.9 %collective-permute-start.3 = (bf16[4,1024,128]{2,1,0:T(8,128)(2,1)S(1)}, bf16[4,1024,128]{2,1,0:T(8,128)(2,1)}, u32[]{:S(2)}, u32[]{:S(2)}) collective-permute-start(bf16[4,1024,128]{2,1,0:T(8,128)(2,1)S(1)} %all-to-all-done.1.a_ref), channel_id=1, source_target_pairs={{0,8},{8,0},{1,9},{9,1},{2,10},{10,2},{3,11},{11,3},{4,12},{12,4},... | collective-permute-start | bytes 3145736 | tf_op jit(solution)/shard_map/ppermute | solution.py:203
  109.2 15.1 %collective-permute-done.4.h1 = bf16[128,4096]{1,0:T(8,128)(2,1)S(1)} collective-permute-done((bf16[128,4096]{1,0:T(8,128)(2,1)S(1)}, bf16[128,4096]{1,0:T(8,128)(2,1)S(1)}, u32[]{:S(2)}, u32[]{:S(2)}) %collective-permute-start.4) | collective-permute-done | bytes 1048608 | tf_op jit(solution)/shard_map/ppermute | solution.py:203
  124.4 19.6 %collective-permute-done.5.h2 = bf16[128,4096]{1,0:T(8,128)(2,1)} collective-permute-done((bf16[128,4096]{1,0:T(8,128)(2,1)S(1)}, bf16[128,4096]{1,0:T(8,128)(2,1)}, u32[]{:S(2)}, u32[]{:S(2)}) %collective-permute-start.5) | collective-permute-done | bytes 1048608 | tf_op jit(solution)/shard_map/ppermute | solution.py:203
  144.0 3.0 %shard_map.93.part_ref = bf16[4,352,128]{2,1,0:T(8,128)(2,1)S(1)} custom-call(s32[3]{0:T(128)S(1)} %pad_add_fusion.place, s32[2]{0:T(128)S(1)} %copy-done.4, bf16[4,1024,128]{2,1,0:T(8,128)(2,1)S(1)} %all-to-all-done.1.a_ref, bf16[128,4096]{1,0:T(8,128)(2,1)S(1)} %reshape.48.h0, bf16[128,4096]{1,0:T(8,128)(2,1)S(1)} %collective-permute-done.4.h1, ...), custom_call_target="tpu_custom_call" | custom-call | flops 402653184 | bytes 5500000 | tf_op jit(solution)/shard_map/pallas_call | solution.py:245
  147.1 4.3 %shard_map.94 = bf16[4,2,352,128]{3,2,1,0:T(8,128)(2,1)} custom-call(s32[3]{0:T(128)S(1)} %pad_add_fusion.place, s32[2]{0:T(128)S(1)} %copy-done.4, bf16[4,1024,128]{2,1,0:T(8,128)(2,1)} %collective-permute-done.3.b_ref, bf16[128,4096]{1,0:T(8,128)(2,1)S(1)} %reshape.48.h0, bf16[128,4096]{1,0:T(8,128)(2,1)S(1)} %collective-permute-done.4.h1, ...), custom_call_target="tpu_custom_call" | custom-call | flops 402653184 | bytes 6500000 | tf_op jit(solution)/shard_map/pallas_call | solution.py:254
  151.3 5.2 %all-to-all-start.2 = ((bf16[4,2,352,128]{3,2,1,0:T(8,128)(2,1)}), bf16[4,2,352,128]{3,2,1,0:T(8,128)(2,1)S(1)}, u32[]{:S(2)}, u32[]{:S(2)}) async-start(bf16[4,2,352,128]{3,2,1,0:T(8,128)(2,1)} %shard_map.94), calls=%async_computation.2 | async-start | bytes 1441792 | tf_op jit(solution)/shard_map/all_to_all | solution.py:263
  156.7 9.0 %all-to-all-done.2.g_ref = bf16[4,2,352,128]{3,2,1,0:T(8,128)(2,1)S(1)} async-done(((bf16[4,2,352,128]{3,2,1,0:T(8,128)(2,1)}), bf16[4,2,352,128]{3,2,1,0:T(8,128)(2,1)S(1)}, u32[]{:S(2)}, u32[]{:S(2)}) %all-to-all-start.2) | async-done | bytes 720928 | tf_op jit(solution)/shard_map/all_to_all | solution.py:263
  165.7 1.1 shard_map.95
  166.8 0.7 reshape.50
  (30 shorter events, 0.9 us)
Async XLA Ops:
  0.1 0.7 copy-start.5
  0.8 1.0 copy-start
  1.8 0.9 copy-start.3
  4.2 27.6 %copy-start.4 = (s32[2]{0:T(128)S(1)}, s32[2]{0:T(128)}, u32[]{:S(2)}) copy-start(s32[2]{0:T(128)} %mine.3) | copy-start | bytes 28
  4.2 85.0 %all-to-all-start = ((bf16[4,448,128]{2,1,0:T(8,128)(2,1)}), bf16[4,448,128]{2,1,0:T(8,128)(2,1)S(1)}, u32[]{:S(2)}, u32[]{:S(2)}) async-start(bf16[4,448,128]{2,1,0:T(8,128)(2,1)} %shard_map.91), calls=%async_computation | async-start | bytes 917504 | tf_op jit(solution)/shard_map/all_to_all | solution.py:229
  31.8 10.7 %collective-permute-start = (s32[2]{0:T(128)S(1)}, s32[2]{0:T(128)S(1)}, u32[]{:S(2)}, u32[]{:S(2)}) collective-permute-start(s32[2]{0:T(128)S(1)} %copy-done.4), channel_id=1, source_target_pairs={{0,256},{256,512},{512,768},{768,0},{1,257},{257,513},{513,769},{7... | collective-permute-start | bytes 32 | tf_op jit(solution)/shard_map/ppermute | solution.py:203
  35.3 7.2 %collective-permute-start.1 = (s32[2]{0:T(128)S(1)}, s32[2]{0:T(128)S(1)}, u32[]{:S(2)}, u32[]{:S(2)}) collective-permute-start(s32[2]{0:T(128)S(1)} %copy-done.4), channel_id=1, source_target_pairs={{0,512},{256,768},{512,0},{768,256},{1,513},{257,769},{513,1},{769... | collective-permute-start | bytes 32 | tf_op jit(solution)/shard_map/ppermute | solution.py:203
  38.1 5.6 %collective-permute-start.2 = (s32[2]{0:T(128)S(1)}, s32[2]{0:T(128)S(1)}, u32[]{:S(2)}, u32[]{:S(2)}) collective-permute-start(s32[2]{0:T(128)S(1)} %copy-done.4), channel_id=1, source_target_pairs={{0,768},{256,0},{512,256},{768,512},{1,769},{257,1},{513,257},{769... | collective-permute-start | bytes 32 | tf_op jit(solution)/shard_map/ppermute | solution.py:203
  90.9 5.0 %copy-start.6 = (bf16[2,16,4,4096]{3,2,1,0:T(4,128)(2,1)S(1)}, bf16[2,16,4,4096]{3,2,1,0:T(4,128)(2,1)}, u32[]{:S(2)}) copy-start(bf16[2,16,4,4096]{3,2,1,0:T(4,128)(2,1)} %param.9) | copy-start | bytes 3145732
  90.9 16.1 %all-to-all-start.1 = ((bf16[4,1024,128]{2,1,0:T(8,128)(2,1)}), bf16[4,1024,128]{2,1,0:T(8,128)(2,1)S(1)}, u32[]{:S(2)}, u32[]{:S(2)}) async-start(bf16[4,1024,128]{2,1,0:T(8,128)(2,1)} %shard_map.92), calls=%async_computation.1 | async-start | bytes 2097152 | tf_op jit(solution)/shard_map/all_to_all | solution.py:233
  95.9 13.0 %copy-start.7 = (f32[1,768]{1,0:T(1,128)S(1)}, f32[1,768]{1,0:T(1,128)}, u32[]{:S(2)}) copy-start(f32[1,768]{1,0:T(1,128)} %param.11) | copy-start | bytes 9220
  96.2 28.2 %collective-permute-start.4 = (bf16[128,4096]{1,0:T(8,128)(2,1)S(1)}, bf16[128,4096]{1,0:T(8,128)(2,1)S(1)}, u32[]{:S(2)}, u32[]{:S(2)}) collective-permute-start(bf16[128,4096]{1,0:T(8,128)(2,1)S(1)} %reshape.48.h0), channel_id=1, source_target_pairs={{0,16},{16,32},{32,48},{48,0},{1,17},{17,33},{33,49},{49,1},{2,18}... | collective-permute-start | bytes 3145736 | tf_op jit(solution)/shard_map/ppermute | solution.py:203
  99.6 44.3 %collective-permute-start.5 = (bf16[128,4096]{1,0:T(8,128)(2,1)S(1)}, bf16[128,4096]{1,0:T(8,128)(2,1)}, u32[]{:S(2)}, u32[]{:S(2)}) collective-permute-start(bf16[128,4096]{1,0:T(8,128)(2,1)S(1)} %reshape.48.h0), channel_id=1, source_target_pairs={{0,48},{16,0},{32,16},{48,32},{1,49},{17,1},{33,17},{49,33},{2,50}... | collective-permute-start | bytes 3145736 | tf_op jit(solution)/shard_map/ppermute | solution.py:203
  103.3 40.7 %collective-permute-start.6 = (bf16[128,4096]{1,0:T(8,128)(2,1)S(1)}, bf16[128,4096]{1,0:T(8,128)(2,1)}, u32[]{:S(2)}, u32[]{:S(2)}) collective-permute-start(bf16[128,4096]{1,0:T(8,128)(2,1)S(1)} %reshape.48.h0), channel_id=1, source_target_pairs={{0,32},{16,48},{32,0},{48,16},{1,33},{17,49},{33,1},{49,17},{2,34}... | collective-permute-start | bytes 3145736 | tf_op jit(solution)/shard_map/ppermute | solution.py:203
  107.0 40.0 %collective-permute-start.3 = (bf16[4,1024,128]{2,1,0:T(8,128)(2,1)S(1)}, bf16[4,1024,128]{2,1,0:T(8,128)(2,1)}, u32[]{:S(2)}, u32[]{:S(2)}) collective-permute-start(bf16[4,1024,128]{2,1,0:T(8,128)(2,1)S(1)} %all-to-all-done.1.a_ref), channel_id=1, source_target_pairs={{0,8},{8,0},{1,9},{9,1},{2,10},{10,2},{3,11},{11,3},{4,12},{12,4},... | collective-permute-start | bytes 3145736 | tf_op jit(solution)/shard_map/ppermute | solution.py:203
  109.2 34.8 %copy-start.1 = (f32[64,128]{1,0:T(8,128)S(1)}, f32[64,128]{1,0:T(8,128)}, u32[]{:S(2)}) copy-start(f32[64,128]{1,0:T(8,128)} %constant.25.clone.cos_ref) | copy-start | bytes 98308
  109.2 34.8 %copy-start.2 = (f32[64,128]{1,0:T(8,128)S(1)}, f32[64,128]{1,0:T(8,128)}, u32[]{:S(2)}) copy-start(f32[64,128]{1,0:T(8,128)} %constant.26.clone.sin_ref) | copy-start | bytes 98308
  151.3 5.2 %copy-start.8 = (s32[2,16]{1,0:T(2,128)S(1)}, s32[2,16]{1,0:T(2,128)}, u32[]{:S(2)}) copy-start(s32[2,16]{1,0:T(2,128)} %param.15) | copy-start | bytes 388
  151.3 14.3 %all-to-all-start.2 = ((bf16[4,2,352,128]{3,2,1,0:T(8,128)(2,1)}), bf16[4,2,352,128]{3,2,1,0:T(8,128)(2,1)S(1)}, u32[]{:S(2)}, u32[]{:S(2)}) async-start(bf16[4,2,352,128]{3,2,1,0:T(8,128)(2,1)} %shard_map.94), calls=%async_computation.2 | async-start | bytes 1441792 | tf_op jit(solution)/shard_map/all_to_all | solution.py:263

commit v2 on v0

--- a/solution.py
+++ b/solution.py
@@ -67,7 +67,7 @@
             out_ref[d, base : base + C_ROWS, :] = zg_ref[p >> 1, src, :]
 
 
-def project(place, core, mine, from_ref, h_refs, bias_ref, cos_ref, sin_ref, wt_ref, put):
+def project(place, core, mine, from_ref, h_ref, bias_ref, cos_ref, sin_ref, wt_ref, put):
     for y in range(NY):
         for z in range(NZ):
             for half in range(2):
@@ -79,11 +79,11 @@
     cosine = cos_ref[at, :]
     sine = sin_ref[at, :]
     bias = bias_ref[core]
-    for h_ref, shift in zip(h_refs, (0, 3, 1, 2)):
-        mixed = lax.dot_general(
-            wt_ref[...], h_ref[...], (((1,), (1,)), ((), ())), preferred_element_type=jnp.float32
-        )
-        mixed = mixed + bias
+    every = lax.dot_general(
+        h_ref[...], wt_ref[...], (((1,), (1,)), ((), ())), preferred_element_type=jnp.float32
+    ).T
+    for k, shift in enumerate((0, 3, 1, 2)):
+        mixed = every[:, k * ROWS : (k + 1) * ROWS] + bias
         to = (place[0] + shift) & 3
         for g in range(HEADS):
             lo = mixed[g * 16 : g * 16 + 8]
@@ -101,30 +101,30 @@
 
 
 def first_kernel(
-    place, mine, a_ref, h0, h1, h2, h3, bias_ref, cos_ref, sin_ref, out_ref, wt_ref
+    place, mine, a_ref, h0, h1, h2, h3, bias_ref, cos_ref, sin_ref, out_ref, h_ref, wt_ref
 ):
     def put(d, rows, value):
         out_ref[d, rows, :] = value
 
-    hs = (h0, h1, h2, h3)
-    project(place, place[1], mine, a_ref, hs, bias_ref, cos_ref, sin_ref, wt_ref, put)
+    for k, ref in enumerate((h0, h1, h2, h3)):
+        h_ref[k * ROWS : (k + 1) * ROWS, :] = ref[...]
+    project(place, place[1], mine, a_ref, h_ref, bias_ref, cos_ref, sin_ref, wt_ref, put)
 
 
 def second_kernel(
-    place, mine, b_ref, h0, h1, h2, h3, bias_ref, cos_ref, sin_ref, part_ref, out_ref, wt_ref
+    place, mine, b_ref, h_ref, bias_ref, cos_ref, sin_ref, part_ref, out_ref, wt_ref
 ):
     c = place[1]
 
     def put(d, rows, value):
         out_ref[d, 1 - c, rows, :] = value
 
-    hs = (h0, h1, h2, h3)
-    project(place, 1 - c, mine, b_ref, hs, bias_ref, cos_ref, sin_ref, wt_ref, put)
+    project(place, 1 - c, mine, b_ref, h_ref, bias_ref, cos_ref, sin_ref, wt_ref, put)
     for d in range(NX):
         out_ref[d, c] = part_ref[d]
 
 
-def attend_kernel(g_ref, live_ref, out_ref, q_ref, kn_ref, vn_ref, kc_ref, vc_ref):
+def attend_kernel(lengths, g_ref, out_ref, q_ref, kn_ref, vn_ref, kc_ref, vc_ref):
     for x in range(NX):
         for g in range(HEADS):
             pair = [g_ref[x, c, g * 16 : g * 16 + 16, :].astype(jnp.float32) for c in range(NC)]
@@ -144,6 +144,12 @@
                 at = slice((x * NC + k) * TOK, (x * NC + k + 1) * TOK)
                 kc_ref[i, at, :] = g_ref[x, k, base : base + TOK, :]
                 vc_ref[i, at, :] = g_ref[x, k, base + TOK : base + 2 * TOK, :]
+    row = lax.broadcasted_iota(jnp.int32, (1, ROWS), 1)
+    live = jnp.zeros((1, ROWS), jnp.int32)
+    for i in range(SLOTS):
+        for k in range(SAMPLES_DEV):
+            live = jnp.where((row >> 2) == i * SAMPLES_DEV + k, lengths[i, k], live)
+    live = (row & 3) < live
     q = q_ref[...]
     scaling = HD ** (-0.5)
     lane = lax.broadcasted_iota(jnp.int32, (1, GROUP * ROWS), 1) & (ROWS - 1)
@@ -172,7 +178,7 @@
     out = out / total
     for h in range(GROUP):
         part = out[:, h * 128 : (h + 1) * 128]
-        part = jnp.where(live_ref[...] > 0, part, 0.0)
+        part = jnp.where(live, part, 0.0)
         out_ref[:, h * 128 : (h + 1) * 128] = part.T.astype(jnp.bfloat16)
 
 
@@ -183,12 +189,14 @@
     return np.cos(angles).astype(np.float32), np.sin(angles).astype(np.float32)
 
 
-def call(kernel, shape, specs, dtype=jnp.bfloat16, scratch=(), flops=0, moved=0, limit=8):
+def call(kernel, shape, specs, scratch=(), flops=0, moved=0, limit=8):
+    many = isinstance(shape, list)
+    shapes = [jax.ShapeDtypeStruct(sh, jnp.bfloat16) for sh in (shape if many else [shape])]
     return pl.pallas_call(
         kernel,
-        out_shape=jax.ShapeDtypeStruct(shape, dtype),
+        out_shape=shapes if many else shapes[0],
         in_specs=specs,
-        out_specs=vmem(),
+        out_specs=[vmem()] * len(shapes) if many else vmem(),
         scratch_shapes=list(scratch),
         cost_estimate=pl.CostEstimate(flops=flops, bytes_accessed=moved, transcendentals=0),
         compiler_params=pltpu.CompilerParams(vmem_limit_bytes=limit * 2**20),
@@ -214,7 +222,7 @@
     wanted = lax.all_to_all(wanted, "y", 0, 0, tiled=True)
 
     sent = call(
-        prep_kernel, (Z_ROWS, 128), [smem(), smem(), vmem(), vmem()], moved=600000
+        prep_kernel, (Z_ROWS, 128), [smem(), smem(), vmem(), vmem()], moved=600000, limit=60
     )(
         place,
         block_table,
@@ -236,9 +244,9 @@
     cosine, sine = jnp.asarray(cosine), jnp.asarray(sine)
     scratch = [pltpu.VMEM((W_ROWS, WIDTH), bf16)]
     flops = 2 * W_ROWS * WIDTH * 4 * ROWS
-    part = call(
+    part, every = call(
         first_kernel,
-        (NX, X_ROWS, 128),
+        [(NX, X_ROWS, 128), (NX * ROWS, WIDTH)],
         [smem(), smem()] + [vmem()] * 8,
         scratch=scratch,
         flops=flops,
@@ -248,20 +256,18 @@
     made = call(
         second_kernel,
         (NX, NC, X_ROWS, 128),
-        [smem(), smem()] + [vmem()] * 9,
+        [smem(), smem()] + [vmem()] * 6,
         scratch=scratch,
         flops=flops,
         moved=6500000,
         limit=16,
-    )(place, group_prompts, b, h0, h1, h2, h3, bias, cosine, sine, part)
+    )(place, group_prompts, b, every, bias, cosine, sine, part)
     got = lax.all_to_all(made, "x", 0, 0, tiled=True)
 
-    step = jnp.arange(STEPS, dtype=jnp.int32)
-    live = (step[None, None, :] < decode_len[:, :, None]).astype(jnp.float32).reshape(1, ROWS)
     out = call(
         attend_kernel,
         (ROWS, GROUP * HD),
-        [vmem(), vmem()],
+        [smem(), vmem()],
         scratch=[
             pltpu.VMEM((HD, GROUP * ROWS), bf16),
             pltpu.VMEM((HD, ROWS), bf16),
@@ -272,7 +278,7 @@
         flops=400000000,
         moved=1000000,
         limit=16,
-    )(got, live)
+    )(decode_len, got)
     return out.reshape(SLOTS, SAMPLES_DEV, STEPS, 1, GROUP * HD)
 
 

time: 149 us -> 148 us (level)
  the two profiles are of different devices: /device:TPU:8 before, /device:TPU:25 now
where the time goes in v2:
time: 148 us; the launch traced here: 146 us
  blocking collectives  73 us (49%)
  waiting for transfers between devices  32.6 us (22%)
  starting transfers between devices  26.5 us (18%)
  Pallas kernels  10.9 us (7%)
  local copies, waits for them, and re-layouts  2.59 us (2%)
    all_gather x1, blocking collectives, step(): zg = lax.all_gather(sent, 'zh', axis=0, tiled=True)  58.2 us
    ppermute x4, waiting for transfers between devices, hop(): lax.ppermute(array, axis, [(i, (i + by) % size) for i in range(size)])  32.6 us
    ppermute x4, starting transfers between devices, hop(): lax.ppermute(array, axis, [(i, (i + by) % size) for i in range(size)])  18.1 us
    all_to_all x1, blocking collectives, step(): got = lax.all_to_all(made, 'x', 0, 0, tiled=True)  14.9 us
    all_to_all x1, starting transfers between devices, step(): a = lax.all_to_all(picked, 'y', 0, 0, tiled=True)  4.24 us
    all_to_all x1, starting transfers between devices, step(): wanted = lax.all_to_all(wanted, 'y', 0, 0, tiled=True)  4.12 us
    pallas_call x1, Pallas kernels, step(): call(first_kernel, [(NX, X_ROWS, 128), (NX * ROWS, WIDTH)], [smem(), smem...  3.01 us
  transfers between devices with their start and end apart: 6, of which 3 were waited for; matrix products, arithmetic and copies ran while one was open for 1% of the time, Pallas kernels for 3%

profile of v2, /device:TPU:25, one launch (start us, length us, event | category | flops | bytes accessed | tf_op | source)
XLA Modules:
  0.0 146.5 jit_solution(15540344260199949650)
XLA Ops:
  0.0 1.3 broadcast_in_dim.6
  1.3 4.1 %all-to-all-start = ((s32[4,1,2]{2,1,0:T(1,128)}), s32[4,1,2]{2,1,0:T(1,128)S(1)}, u32[]{:S(2)}, u32[]{:S(2)}) async-start(s32[4,1,2]{2,1,0:T(1,128)} %broadcast_in_dim.6), calls=%async_computation | async-start | bytes 4096 | tf_op jit(solution)/shard_map/all_to_all | solution.py:222
  5.5 0.6 pad_add_fusion.place
  6.1 1.9 %shard_map.91 = bf16[448,128]{1,0:T(8,128)(2,1)} custom-call(s32[2]{0:T(128)} %pad_add_fusion.place, s32[2,4]{1,0:T(2,128)} %table.1, bf16[256,768]{1,0:T(8,128)(2,1)} %bitcast.14, bf16[2,6,16,256]{3,2,1,0:T(8,128)(2,1)} %bitcast.15), custom_call_target="tpu_custom_call" | custom-call | bytes 600000 | tf_op jit(solution)/shard_map/pallas_call | solution.py:224
  8.0 58.2 %all_gather.3 = bf16[1792,128]{1,0:T(8,128)(2,1)S(1)} all-gather(bf16[448,128]{1,0:T(8,128)(2,1)} %shard_map.91), channel_id=1, replica_groups=mesh['y'=4,'zh'=4,'x'=4,'c'=2,'tp'=8] {'zh'}, dimensions={0}, use_global_device_ids=true | all-gather | bytes 573440 | tf_op jit(solution)/shard_map/all_gather | solution.py:232
  66.1 1.7 %shard_map.92 = bf16[4,1024,128]{2,1,0:T(8,128)(2,1)} custom-call(s32[4,2]{1,0:T(4,128)S(1)} %bitcast.13, bf16[4,448,128]{2,1,0:T(8,128)(2,1)S(1)} %bitcast.12), custom_call_target="tpu_custom_call" | custom-call | bytes 1500000 | tf_op jit(solution)/shard_map/pallas_call | solution.py:234
  67.8 4.2 %all-to-all-start.1 = ((bf16[4,1024,128]{2,1,0:T(8,128)(2,1)}), bf16[4,1024,128]{2,1,0:T(8,128)(2,1)S(1)}, u32[]{:S(2)}, u32[]{:S(2)}) async-start(bf16[4,1024,128]{2,1,0:T(8,128)(2,1)} %shard_map.92), calls=%async_computation.1 | async-start | bytes 2097152 | tf_op jit(solution)/shard_map/all_to_all | solution.py:235
  72.0 0.3 reshape.29.h0
  72.3 4.8 %collective-permute-start.3 = (bf16[128,4096]{1,0:T(8,128)(2,1)S(1)}, bf16[128,4096]{1,0:T(8,128)(2,1)S(1)}, u32[]{:S(2)}, u32[]{:S(2)}) collective-permute-start(bf16[128,4096]{1,0:T(8,128)(2,1)S(1)} %reshape.29.h0), channel_id=1, source_target_pairs={{0,32},{16,48},{32,0},{48,16},{1,33},{17,49},{33,1},{49,17},{2,34}... | collective-permute-start | bytes 3145736 | tf_op jit(solution)/shard_map/ppermute | solution.py:208
  77.1 2.8 %collective-permute-start.2 = (bf16[128,4096]{1,0:T(8,128)(2,1)S(1)}, bf16[128,4096]{1,0:T(8,128)(2,1)}, u32[]{:S(2)}, u32[]{:S(2)}) collective-permute-start(bf16[128,4096]{1,0:T(8,128)(2,1)S(1)} %reshape.29.h0), channel_id=1, source_target_pairs={{0,48},{16,0},{32,16},{48,32},{1,49},{17,1},{33,17},{49,33},{2,50}... | collective-permute-start | bytes 3145736 | tf_op jit(solution)/shard_map/ppermute | solution.py:208
  79.9 2.5 %collective-permute-start.1 = (bf16[128,4096]{1,0:T(8,128)(2,1)S(1)}, bf16[128,4096]{1,0:T(8,128)(2,1)}, u32[]{:S(2)}, u32[]{:S(2)}) collective-permute-start(bf16[128,4096]{1,0:T(8,128)(2,1)S(1)} %reshape.29.h0), channel_id=1, source_target_pairs={{0,16},{16,32},{32,48},{48,0},{1,17},{17,33},{33,49},{49,1},{2,18}... | collective-permute-start | bytes 3145736 | tf_op jit(solution)/shard_map/ppermute | solution.py:208
  82.4 8.0 %collective-permute-start = (bf16[4,1024,128]{2,1,0:T(8,128)(2,1)S(1)}, bf16[4,1024,128]{2,1,0:T(8,128)(2,1)}, u32[]{:S(2)}, u32[]{:S(2)}) collective-permute-start(bf16[4,1024,128]{2,1,0:T(8,128)(2,1)S(1)} %all-to-all-done.1.a_ref), channel_id=1, source_target_pairs={{0,8},{8,0},{1,9},{9,1},{2,10},{10,2},{3,11},{11,3},{4,12},{12,4},... | collective-permute-start | bytes 3145736 | tf_op jit(solution)/shard_map/ppermute | solution.py:208
  90.5 0.1 reshape.30
  90.7 0.1 broadcast_in_dim.14
  90.7 4.3 %collective-permute-done.3.h3 = bf16[128,4096]{1,0:T(8,128)(2,1)S(1)} collective-permute-done((bf16[128,4096]{1,0:T(8,128)(2,1)S(1)}, bf16[128,4096]{1,0:T(8,128)(2,1)S(1)}, u32[]{:S(2)}, u32[]{:S(2)}) %collective-permute-start.3) | collective-permute-done | bytes 1048608 | tf_op jit(solution)/shard_map/ppermute | solution.py:208
  95.0 27.5 %collective-permute-done.2.h2 = bf16[128,4096]{1,0:T(8,128)(2,1)} collective-permute-done((bf16[128,4096]{1,0:T(8,128)(2,1)S(1)}, bf16[128,4096]{1,0:T(8,128)(2,1)}, u32[]{:S(2)}, u32[]{:S(2)}) %collective-permute-start.2) | collective-permute-done | bytes 1048608 | tf_op jit(solution)/shard_map/ppermute | solution.py:208
  122.5 0.9 collective-permute-done.1.h1
  123.4 0.1 broadcast_in_dim.15.bias_ref
  123.5 3.0 %shard_map.93 = (bf16[4,352,128]{2,1,0:T(8,128)(2,1)S(1)}, bf16[512,4096]{1,0:T(8,128)(2,1)S(1)}) custom-call(s32[2]{0:T(128)S(1)} %copy-done.3, s32[2]{0:T(128)S(1)} %copy-done.2, bf16[4,1024,128]{2,1,0:T(8,128)(2,1)S(1)} %all-to-all-done.1.a_ref, bf16[128,4096]{1,0:T(8,128)(2,1)S(1)} %reshape.29.h0, bf16[128,4096]{1,0:T(8,128)(2,1)} %collective-permute-done.1.h1, ...), custom_call_target="tpu_custom_call" | custom-call | flops 402653184 | bytes 5500000 | tf_op jit(solution)/shard_map/pallas_call | solution.py:247
  126.5 0.0 copy-start.4
  126.5 2.7 %shard_map.94 = bf16[4,2,352,128]{3,2,1,0:T(8,128)(2,1)S(1)} custom-call(s32[2]{0:T(128)S(1)} %copy-done.3, s32[2]{0:T(128)S(1)} %copy-done.2, bf16[4,1024,128]{2,1,0:T(8,128)(2,1)} %collective-permute-done.b_ref, bf16[512,4096]{1,0:T(8,128)(2,1)S(1)} %get-tuple-element.7.h_ref, f32[2,96,128]{2,1,0:T(8,128)S(1)} %broadcast_in_dim.15.bias_ref, ...), custom_call_target="tpu_custom_call" | custom-call | flops 402653184 | bytes 6500000 | tf_op jit(solution)/shard_map/pallas_call | solution.py:256
  129.2 14.9 %all_to_all.18.g_ref = bf16[4,2,352,128]{3,2,1,0:T(8,128)(2,1)S(1)} all-to-all(bf16[4,2,352,128]{3,2,1,0:T(8,128)(2,1)S(1)} %shard_map.94), channel_id=1, replica_groups=mesh['y'=4,'zh'=4,'x'=4,'c'=2,'tp'=8] {'x'}, dimensions={0} | all-to-all | bytes 1441792 | tf_op jit(solution)/shard_map/all_to_all | solution.py:265
  144.1 1.7 %shard_map.95 = bf16[128,512]{1,0:T(8,128)(2,1)S(1)} custom-call(s32[2,16]{1,0:T(2,128)S(1)} %copy-done.4, bf16[4,2,352,128]{3,2,1,0:T(8,128)(2,1)S(1)} %all_to_all.18.g_ref), custom_call_target="tpu_custom_call" | custom-call | flops 400000000 | bytes 1000000 | tf_op jit(solution)/shard_map/pallas_call | solution.py:267
  145.8 0.7 reshape.31
  (19 shorter events, 0.1 us)
Async XLA Ops:
  0.0 123.5 %copy-start = (f32[64,128]{1,0:T(8,128)S(1)}, f32[64,128]{1,0:T(8,128)}, u32[]{:S(2)}) copy-start(f32[64,128]{1,0:T(8,128)} %constant.22.clone.sin_ref) | copy-start | bytes 98308
  0.0 123.5 %copy-start.1 = (f32[64,128]{1,0:T(8,128)S(1)}, f32[64,128]{1,0:T(8,128)}, u32[]{:S(2)}) copy-start(f32[64,128]{1,0:T(8,128)} %constant.21.clone.cos_ref) | copy-start | bytes 98308
  0.0 123.5 %copy-start.2 = (s32[2]{0:T(128)S(1)}, s32[2]{0:T(128)}, u32[]{:S(2)}) copy-start(s32[2]{0:T(128)} %mine.3) | copy-start | bytes 28
  0.0 72.0 %copy-start.5 = (bf16[2,16,4,4096]{3,2,1,0:T(4,128)(2,1)S(1)}, bf16[2,16,4,4096]{3,2,1,0:T(4,128)(2,1)}, u32[]{:S(2)}) copy-start(bf16[2,16,4,4096]{3,2,1,0:T(4,128)(2,1)} %param.9) | copy-start | bytes 3145732
  0.0 90.4 %copy-start.6 = (f32[1,768]{1,0:T(1,128)S(1)}, f32[1,768]{1,0:T(1,128)}, u32[]{:S(2)}) copy-start(f32[1,768]{1,0:T(1,128)} %param.11) | copy-start | bytes 9220
  1.3 64.8 %all-to-all-start = ((s32[4,1,2]{2,1,0:T(1,128)}), s32[4,1,2]{2,1,0:T(1,128)S(1)}, u32[]{:S(2)}, u32[]{:S(2)}) async-start(s32[4,1,2]{2,1,0:T(1,128)} %broadcast_in_dim.6), calls=%async_computation | async-start | bytes 4096 | tf_op jit(solution)/shard_map/all_to_all | solution.py:222
  6.1 117.4 %copy-start.3 = (s32[2]{0:T(128)S(1)}, s32[2]{0:T(128)}, u32[]{:S(2)}) copy-start(s32[2]{0:T(128)} %pad_add_fusion.place) | copy-start | bytes 28
  67.8 14.6 %all-to-all-start.1 = ((bf16[4,1024,128]{2,1,0:T(8,128)(2,1)}), bf16[4,1024,128]{2,1,0:T(8,128)(2,1)S(1)}, u32[]{:S(2)}, u32[]{:S(2)}) async-start(bf16[4,1024,128]{2,1,0:T(8,128)(2,1)} %shard_map.92), calls=%async_computation.1 | async-start | bytes 2097152 | tf_op jit(solution)/shard_map/all_to_all | solution.py:235
  72.3 22.7 %collective-permute-start.3 = (bf16[128,4096]{1,0:T(8,128)(2,1)S(1)}, bf16[128,4096]{1,0:T(8,128)(2,1)S(1)}, u32[]{:S(2)}, u32[]{:S(2)}) collective-permute-start(bf16[128,4096]{1,0:T(8,128)(2,1)S(1)} %reshape.29.h0), channel_id=1, source_target_pairs={{0,32},{16,48},{32,0},{48,16},{1,33},{17,49},{33,1},{49,17},{2,34}... | collective-permute-start | bytes 3145736 | tf_op jit(solution)/shard_map/ppermute | solution.py:208
  77.1 45.4 %collective-permute-start.2 = (bf16[128,4096]{1,0:T(8,128)(2,1)S(1)}, bf16[128,4096]{1,0:T(8,128)(2,1)}, u32[]{:S(2)}, u32[]{:S(2)}) collective-permute-start(bf16[128,4096]{1,0:T(8,128)(2,1)S(1)} %reshape.29.h0), channel_id=1, source_target_pairs={{0,48},{16,0},{32,16},{48,32},{1,49},{17,1},{33,17},{49,33},{2,50}... | collective-permute-start | bytes 3145736 | tf_op jit(solution)/shard_map/ppermute | solution.py:208
  79.9 43.5 %collective-permute-start.1 = (bf16[128,4096]{1,0:T(8,128)(2,1)S(1)}, bf16[128,4096]{1,0:T(8,128)(2,1)}, u32[]{:S(2)}, u32[]{:S(2)}) collective-permute-start(bf16[128,4096]{1,0:T(8,128)(2,1)S(1)} %reshape.29.h0), channel_id=1, source_target_pairs={{0,16},{16,32},{32,48},{48,0},{1,17},{17,33},{33,49},{49,1},{2,18}... | collective-permute-start | bytes 3145736 | tf_op jit(solution)/shard_map/ppermute | solution.py:208
  82.4 44.1 %collective-permute-start = (bf16[4,1024,128]{2,1,0:T(8,128)(2,1)S(1)}, bf16[4,1024,128]{2,1,0:T(8,128)(2,1)}, u32[]{:S(2)}, u32[]{:S(2)}) collective-permute-start(bf16[4,1024,128]{2,1,0:T(8,128)(2,1)S(1)} %all-to-all-done.1.a_ref), channel_id=1, source_target_pairs={{0,8},{8,0},{1,9},{9,1},{2,10},{10,2},{3,11},{11,3},{4,12},{12,4},... | collective-permute-start | bytes 3145736 | tf_op jit(solution)/shard_map/ppermute | solution.py:208
  126.5 17.6 %copy-start.4 = (s32[2,16]{1,0:T(2,128)S(1)}, s32[2,16]{1,0:T(2,128)}, u32[]{:S(2)}) copy-start(s32[2,16]{1,0:T(2,128)} %lengths.1) | copy-start | bytes 388
